TPU v7x, 128 devices: a whole 4x4x4 slice. The times are simulated.
128 devices in a mesh: corpus: 16 (over z, y), fsdp: 2 (over core), tensor: 4 (over x).
Axes of the slice: x: 4, y: 4, z: 4, core: 2. Of those that a mesh axis runs over, the one named last changes fastest.
Arguments:
- queries_in: bfloat16 [4096, 4096], P(('corpus', 'fsdp')), may hold values from -6 to 6
- head_weight: bfloat16 [4096, 4096], P('fsdp', 'tensor'), may hold values from -0.09375 to 0.09375
- passages: bfloat16 [16384, 4096], P('corpus', 'tensor'), may hold values from -0.15625 to 0.15625
- teacher: float32 [4096, 4, 32], P(('corpus', 'fsdp')), may hold values from -250 to 400
- cand_block: int32 [4096, 4], P(('corpus', 'fsdp')), may hold values from 0 to 127, all different within a row; in each aligned block of 128 rows (0 to 127, 128 to 255, ...) at most 6 rows name the same one
- cand_offset: int32 [4096, 4, 32], P(('corpus', 'fsdp')), may hold values from 0 to 127, as said below
- block_slot: int32 [128], replicated, may hold values from 0 to 127, each once
Outputs:
- kl_loss: float32 [4096], P(('corpus', 'fsdp'))
- head_grad: float32 [4096, 4096], P('fsdp', 'tensor')
Inputs may be any that keep to these rules, and one draw needn't show every extreme that they name: `cand_block`: in the rows of one device no block id appears more than 6 times, and some block id appears exactly 6 times there; the 4 ids of one query differ. `cand_offset`: the 32 offsets of one query in one block differ. `block_slot`: each storage position is taken by exactly one block.
All inputs are finite; a program needn't handle non-finite values.
Results may differ from a plain program's by a relative error of at most 0.012.
The roundings to bfloat16 on the way count: a program that leaves them out, or rounds other values in their place, can miss the bound.
Values may be sent and summed in bfloat16 or wider, within the bound.
A program may use at most 128 MiB of HBM per device.

v0:
```python
import jax
import jax.numpy as jnp
from jax import lax
from jax.sharding import PartitionSpec as P

ROWS = 128
MOSTB = 6


def on_device(queries_in, head_weight, passages, teacher, cand_block, cand_offset, block_slot):
    query_rows, model_width = queries_in.shape
    head_cols = head_weight.shape[1]
    per_query = cand_block.shape[1]
    offset_count = cand_offset.shape[2]
    total_blocks = block_slot.shape[0]
    n_corpus = lax.axis_size("corpus")
    blocks_here = passages.shape[0] // ROWS
    capacity = MOSTB
    slot_total = total_blocks * capacity
    columns = queries_in
    query = jnp.dot(
        columns,
        lax.all_gather(head_weight, "fsdp", axis=0, tiled=True),
        preferred_element_type=jnp.float32,
    ).astype(jnp.bfloat16)
    block_ids = lax.broadcasted_iota(jnp.int32, (1, total_blocks), 1)
    named = (cand_block.reshape(-1, 1) == block_ids).astype(jnp.int32)
    slot_of = jnp.sum(named * block_slot.reshape(1, -1), axis=1)
    slot_hits = (slot_of[:, None] == block_ids).astype(jnp.int32)
    slot_rank = jnp.sum((jnp.cumsum(slot_hits, axis=0) - slot_hits) * slot_hits, axis=1)
    position = slot_of * capacity + slot_rank
    query_copies = jnp.repeat(query, per_query, axis=0)
    send_queries = jnp.zeros((slot_total, head_cols), jnp.bfloat16).at[position].set(query_copies)
    send_queries = send_queries.reshape(n_corpus, blocks_here, capacity, head_cols)
    offset_rows = cand_offset.reshape(-1, offset_count)
    send_offsets = jnp.zeros((slot_total, offset_count), jnp.int32).at[position].set(offset_rows)
    send_offsets = send_offsets.reshape(n_corpus, blocks_here, capacity, offset_count)
    embedded = passages.reshape(blocks_here, ROWS, head_cols)
    scores = jnp.einsum(
        "sjmd,jrd->sjmr",
        lax.all_to_all(send_queries, "corpus", split_axis=0, concat_axis=0, tiled=True),
        embedded,
        preferred_element_type=jnp.float32,
    )
    returned_scores = lax.all_to_all(scores, "corpus", split_axis=0, concat_axis=0, tiled=True)
    picked = returned_scores.reshape(slot_total, ROWS)[position].reshape(
        query_rows, per_query, ROWS
    )
    partial_scores = jnp.take_along_axis(picked, cand_offset, axis=2)
    student = 50.0 * lax.psum(partial_scores, "tensor")
    log_student = student - jax.nn.logsumexp(student, axis=(1, 2), keepdims=True)
    log_teacher = teacher - jax.nn.logsumexp(teacher, axis=(1, 2), keepdims=True)
    prob_teacher = jnp.exp(log_teacher)
    kl_loss = jnp.sum(prob_teacher * (log_teacher - log_student), axis=(1, 2))
    dscore = (50.0 * (jnp.exp(log_student) - prob_teacher)).astype(jnp.bfloat16)
    flat_index = (position[:, None] * ROWS + offset_rows).reshape(-1)
    dense_grad = (
        jnp.zeros((slot_total * ROWS,), jnp.bfloat16).at[flat_index].set(dscore.reshape(-1))
    )
    dense_grad = dense_grad.reshape(n_corpus, blocks_here, capacity, ROWS)
    block_part = jnp.einsum(
        "sjmr,jrd->sjmd",
        lax.all_to_all(dense_grad, "corpus", split_axis=0, concat_axis=0, tiled=True),
        embedded,
        preferred_element_type=jnp.float32,
    ).astype(jnp.bfloat16)
    arrived_parts = lax.all_to_all(block_part, "corpus", split_axis=0, concat_axis=0, tiled=True)
    parts = arrived_parts.reshape(slot_total, head_cols)[position].reshape(
        query_rows, per_query, head_cols
    )
    query_grad = jnp.sum(parts.astype(jnp.float32), axis=1).astype(jnp.bfloat16)
    columns = queries_in
    grad_share = lax.psum_scatter(
        lax.dot_general(
            columns, query_grad, (((0,), (0,)), ((), ())), preferred_element_type=jnp.float32
        ),
        "fsdp",
        scatter_dimension=0,
        tiled=True,
    )
    head_grad = lax.psum(grad_share, "corpus")
    return (kl_loss, head_grad)


def solution(mesh):
    placed = (
        P(("corpus", "fsdp"), None),
        P("fsdp", "tensor"),
        P("corpus", "tensor"),
        P(("corpus", "fsdp"), None, None),
        P(("corpus", "fsdp"), None),
        P(("corpus", "fsdp"), None, None),
        P(),
    )
    return jax.shard_map(
        on_device,
        mesh=mesh,
        in_specs=placed,
        out_specs=(P(("corpus", "fsdp")), P("fsdp", "tensor")),
        check_vma=False,
    )
```

profile of v0, /device:TPU:0, one launch (start us, length us, event | category | flops | bytes accessed | tf_op | source)
XLA Modules:
  0.0 656.1 jit_solution(10483691207682673269)
XLA Ops:
  9.6 0.8 reshape.163
  10.5 24.3 %all-gather.2.cloned.1.call-done = bf16[4096,1024]{1,0:T(8,128)(2,1)} async-done(((bf16[2048,1024]{1,0:T(8,128)(2,1)}), bf16[4096,1024]{1,0:T(8,128)(2,1)}) %all-gather.2.cloned.1.call-update) | async-done | bytes 8388624 | tf_op jit(solution)/shard_map/all_gather | solution.py:23
  34.7 4.6 convolution_convert_fusion.1
  39.7 1.1 reshape.194
  40.8 4.5 scatter_custom_fusion
  45.3 3.7 reshape.158
  49.0 3.8 copy.62
  52.8 7.1 %all-to-all-start = ((bf16[16,8,6,1024]{3,1,2,0:T(8,128)(2,1)}), bf16[16,8,6,1024]{3,1,2,0:T(8,128)(2,1)}, u32[]{:S(2)}, u32[]{:S(2)}) async-start(bf16[16,8,6,1024]{3,1,2,0:T(8,128)(2,1)} %copy.62), calls=%async_computation | async-start | bytes 3145728 | tf_op jit(solution)/shard_map/all_to_all | solution.py:41
  60.6 24.8 %all-to-all-done = bf16[16,8,6,1024]{3,1,2,0:T(8,128)(2,1)} async-done(((bf16[16,8,6,1024]{3,1,2,0:T(8,128)(2,1)}), bf16[16,8,6,1024]{3,1,2,0:T(8,128)(2,1)}, u32[]{:S(2)}, u32[]{:S(2)}) %all-to-all-start) | async-done | bytes 1572896 | tf_op jit(solution)/shard_map/all_to_all | solution.py:41
  85.4 2.6 fusion.3
  88.1 1.0 copy.64
  89.0 3.6 all-to-all-start.1
  93.1 9.3 %all-to-all-done.1 = f32[16,8,6,128]{3,1,2,0:T(8,128)S(1)} async-done(((f32[16,8,6,128]{3,1,2,0:T(8,128)}), f32[16,8,6,128]{3,1,2,0:T(8,128)S(1)}, u32[]{:S(2)}, u32[]{:S(2)}) %all-to-all-start.1) | async-done | bytes 393248 | tf_op jit(solution)/shard_map/all_to_all | solution.py:45
  102.6 1.0 gather_fusion
  103.6 145.8 %gather_fusion.2 = f32[16384]{0:T(1024)S(1)} fusion(f32[128,4,128]{2,1,0:T(4,128)S(1)} %bitcast.43, s32[16384]{0:T(1024)S(1)} %reshape.184), kind=kCustom, calls=%fused_computation.2 | custom fusion | bytes 327680 | tf_op jit(solution)/shard_map/jit(take_along_axis)/gather | solution.py:49
  250.7 38.4 %all-reduce.3.cloned.1.call-done = f32[128,4,32]{0,2,1:T(8,128)} async-done(((f32[128,4,32]{0,2,1:T(8,128)}), f32[128,4,32]{0,2,1:T(8,128)}) %all-reduce.3.cloned.1.call-update) | async-done | bytes 65552 | tf_op jit(solution)/shard_map/psum | solution.py:50
  289.1 0.9 multiply_reduce_fusion.1
  289.9 0.9 exponential_reduce_fusion
  290.8 1.4 multiply_convert_fusion
  292.5 112.7 %scatter_custom_fusion.1 = bf16[98304]{0:T(1024)(128)(2,1)S(1)} fusion(s32[16384]{0:T(1024)} %bitcast.46, bf16[16384]{0:T(1024)(128)(2,1)S(1)} %reshape.202, bf16[]{:T(256)} %constant.17.clone.1), kind=kCustom, calls=%fused_computation.28 | custom fusion | bytes 197120 | tf_op jit(solution)/shard_map/scatter | solution.py:58
  405.4 15.1 %all_to_all.20 = bf16[16,8,6,128]{3,1,2,0:T(8,128)(2,1)S(1)} all-to-all(bf16[16,8,6,128]{3,1,2,0:T(8,128)(2,1)S(1)} %copy.70), channel_id=1, replica_groups=mesh['corpus'=16,'fsdp'=2,'tensor'=4] {'corpus'}, dimensions={0} | all-to-all | bytes 393216 | tf_op jit(solution)/shard_map/all_to_all | solution.py:63
  421.0 0.9 copy.72
  421.9 22.4 %all_to_all.21 = bf16[16,8,6,1024]{3,1,2,0:T(8,128)(2,1)S(1)} all-to-all(bf16[16,8,6,1024]{3,1,2,0:T(8,128)(2,1)S(1)} %copy.72), channel_id=1, replica_groups=mesh['corpus'=16,'fsdp'=2,'tensor'=4] {'corpus'}, dimensions={0} | all-to-all | bytes 3145728 | tf_op jit(solution)/shard_map/all_to_all | solution.py:67
  444.3 2.4 copy.73
  446.7 3.7 reshape.166
  450.5 5.1 gather_fusion.1
  455.6 2.3 reshape.167
  457.9 2.5 reduce_sum.62
  460.4 8.1 %convolution_bitcast_fusion = f32[4096,1024]{0,1:T(8,128)} fusion(bf16[128,1024]{1,0:T(8,128)(2,1)S(1)} %reduce_sum.62, bf16[128,4096]{1,0:T(8,128)(2,1)S(1)} %copy-done.2), kind=kOutput, calls=%fused_computation.5 | convolution fusion | flops 1073741824 | bytes 18087936 | tf_op jit(solution)/shard_map/dot_general | solution.py:74
  468.6 24.9 %reduce-scatter.2.cloned.1.call-done = f32[2048,1024]{0,1:T(8,128)} async-done(((f32[4096,1024]{0,1:T(8,128)}), f32[2048,1024]{0,1:T(8,128)}) %reduce-scatter.2.cloned.1.call-update) | async-done | bytes 8388624 | tf_op jit(solution)/shard_map/reduce_scatter | solution.py:73
  493.5 146.8 %all-reduce.5.cloned.1.call-done = f32[2048,1024]{0,1:T(8,128)} async-done(((f32[2048,1024]{0,1:T(8,128)}), f32[2048,1024]{0,1:T(8,128)}) %all-reduce.5.cloned.1.call-update) | async-done | bytes 8388624 | tf_op jit(solution)/shard_map/psum | solution.py:81
  640.4 9.2 %copy.74 = f32[2048,1024]{1,0:T(8,128)} copy(f32[2048,1024]{0,1:T(8,128)} %all-reduce.5.cloned.1.call-done) | data formatting | bytes 16777216
  (63 shorter events, 6.2 us)
Async XLA Ops:
  7.2 78.2 %copy-start = (bf16[1024,1024]{1,0:T(8,128)(2,1)S(1)}, bf16[1024,1024]{1,0:T(8,128)(2,1)}, u32[]{:S(2)}) copy-start(bf16[1024,1024]{1,0:T(8,128)(2,1)} %param.9) | copy-start | bytes 6291460
  7.2 0.8 copy-start.6
  7.2 1.0 copy-start.7
  7.2 2.3 copy-start.3
  7.2 27.5 %copy-start.1 = (bf16[128,4096]{1,0:T(8,128)(2,1)S(1)}, bf16[128,4096]{1,0:T(8,128)(2,1)}, u32[]{:S(2)}) copy-start(bf16[128,4096]{1,0:T(8,128)(2,1)} %param.7) | copy-start | bytes 3145732
  7.2 27.5 %all-gather.2.cloned.1.call-start = ((), (), s32[]{:S(2)}) async-start(), calls=%async_computation.5 | async-start | bytes 12582912 | tf_op jit(solution)/shard_map/all_gather | solution.py:23
  49.0 10.9 %copy-start.5 = (s32[16384,1]{0,1:T(1,128)S(1)}, s32[16384,1]{0,1:T(1,128)}, u32[]{:S(2)}) copy-start(s32[16384,1]{0,1:T(1,128)} %reshape.163) | copy-start | bytes 196612
  52.8 32.6 %all-to-all-start = ((bf16[16,8,6,1024]{3,1,2,0:T(8,128)(2,1)}), bf16[16,8,6,1024]{3,1,2,0:T(8,128)(2,1)}, u32[]{:S(2)}, u32[]{:S(2)}) async-start(bf16[16,8,6,1024]{3,1,2,0:T(8,128)(2,1)} %copy.62), calls=%async_computation | async-start | bytes 3145728 | tf_op jit(solution)/shard_map/all_to_all | solution.py:41
  85.4 7.6 %copy-start.4 = (f32[128,4,32]{0,2,1:T(8,128)S(1)}, f32[128,4,32]{0,2,1:T(8,128)}, u32[]{:S(2)}) copy-start(f32[128,4,32]{0,2,1:T(8,128)} %param.10) | copy-start | bytes 196612
  89.0 13.4 %all-to-all-start.1 = ((f32[16,8,6,128]{3,1,2,0:T(8,128)}), f32[16,8,6,128]{3,1,2,0:T(8,128)S(1)}, u32[]{:S(2)}, u32[]{:S(2)}) async-start(f32[16,8,6,128]{3,1,2,0:T(8,128)} %copy.64), calls=%async_computation.1 | async-start | bytes 786432 | tf_op jit(solution)/shard_map/all_to_all | solution.py:45
  92.6 196.5 %all-reduce.3.cloned.1.call-start = ((), (), s32[]{:S(2)}) async-start(), calls=%async_computation.6 | async-start | bytes 131072 | tf_op jit(solution)/shard_map/psum | solution.py:50
  250.4 243.1 %reduce-scatter.2.cloned.1.call-start = ((), (), s32[]{:S(2)}) async-start(), calls=%async_computation.7 | async-start | bytes 25165824 | tf_op jit(solution)/shard_map/reduce_scatter | solution.py:73
  455.6 4.9 copy-start.2
  468.5 171.8 %all-reduce.5.cloned.1.call-start = ((), (), s32[]{:S(2)}) async-start(), calls=%async_computation.8 | async-start | bytes 16777216 | tf_op jit(solution)/shard_map/psum | solution.py:81
Sparse Core Ops, SparseCore 0:
  9.7 25.0 all-gather.1
  250.6 38.4 all-reduce.2
  468.6 24.7 reduce-scatter.1
  497.0 143.3 all-reduce.4
where the time goes:
time: 657 us; the launch traced here: 656 us
  local copies, waits for them, and re-layouts  300 us (46%)
  waiting for transfers between devices  269 us (41%)
  blocking collectives  37.5 us (6%)
  matrix products  15.9 us (2%)
  between operations  14.1 us (2%)
  starting transfers between devices  11 us (2%)
  other arithmetic  7.89 us (1%)
    psum x1, waiting for transfers between devices, on_device(): head_grad = lax.psum(grad_share, 'corpus')  147 us
    gather x5, local copies, waits for them, and re-layouts, on_device(): partial_scores = jnp.take_along_axis(picked, cand_offset, axis=2)  146 us
    scatter x1, local copies, waits for them, and re-layouts, on_device(): jnp.zeros((slot_total * ROWS,), jnp.bfloat16).at[flat_index]  113 us
    psum x1, waiting for transfers between devices, on_device(): student = 50.0 * lax.psum(partial_scores, 'tensor')  38.4 us
    reduce_scatter x1, waiting for transfers between devices, on_device(): lax.psum_scatter(lax.dot_general(columns, query_grad, (((0,), (0,)), ((),...  24.9 us
    all_to_all x1, waiting for transfers between devices, on_device(): lax.all_to_all(send_queries, 'corpus', split_axis=0, concat_axis=0, tiled...  24.8 us
    all_gather x1, waiting for transfers between devices, on_device(): lax.all_gather(head_weight, 'fsdp', axis=0, tiled=True)  24.3 us
    all_to_all x1, blocking collectives, on_device(): lax.all_to_all(block_part, 'corpus', split_axis=0, concat_axis=0, tiled=T...  22.4 us
  transfers between devices with their start and end apart: 6, of which 6 were waited for; matrix products, arithmetic and copies ran while one was open for 1% of the time, Pallas kernels for 0%

commit v1 on v0

v1 whole, which is shorter than its diff:
```python
import jax
import jax.numpy as jnp
from jax import lax
from jax.sharding import PartitionSpec as P

ROWS = 128
MOSTB = 6
SWAP = [(0, 1), (1, 0)]


def on_device(queries_in, head_weight, passages, teacher, cand_block, cand_offset, block_slot):
    query_rows, width = queries_in.shape
    half = width // 2
    cols = head_weight.shape[1]
    per_query = cand_block.shape[1]
    offset_count = cand_offset.shape[2]
    total_blocks = block_slot.shape[0]
    n_corpus = lax.axis_size("corpus")
    blocks_here = passages.shape[0] // ROWS
    slot_total = total_blocks * MOSTB
    slots_each = blocks_here * MOSTB
    picks = query_rows * per_query
    first = lax.axis_index("fsdp") == 0

    low, high = queries_in[:, :half], queries_in[:, half:]
    mine = jnp.where(first, low, high)
    other = jnp.where(first, high, low)
    theirs = lax.ppermute(other, "fsdp", SWAP)
    part_theirs = jnp.dot(theirs, head_weight, preferred_element_type=jnp.float32)
    back = lax.ppermute(part_theirs, "fsdp", SWAP)
    part_mine = jnp.dot(mine, head_weight, preferred_element_type=jnp.float32)
    query = (part_mine + back).astype(jnp.bfloat16)
    all_mine = lax.all_gather(mine, "corpus", axis=0, tiled=True)
    all_theirs = lax.all_gather(theirs, "corpus", axis=0, tiled=True)

    block_ids = lax.broadcasted_iota(jnp.int32, (1, total_blocks), 1)
    named = (cand_block.reshape(-1, 1) == block_ids).astype(jnp.int32)
    slot_of = jnp.sum(named * block_slot.reshape(1, -1), axis=1)
    hits = slot_of[:, None] == block_ids
    before = (
        lax.broadcasted_iota(jnp.int32, (picks, picks), 1)
        < lax.broadcasted_iota(jnp.int32, (picks, picks), 0)
    ).astype(jnp.bfloat16)
    earlier = jnp.dot(before, hits.astype(jnp.bfloat16), preferred_element_type=jnp.float32)
    slot_rank = jnp.sum(jnp.where(hits, earlier, 0.0), axis=1).astype(jnp.int32)
    position = slot_of * MOSTB + slot_rank

    slot_ids = lax.broadcasted_iota(jnp.int32, (slot_total, 1), 0)
    place = (slot_ids == position.reshape(1, -1)).astype(jnp.bfloat16)
    by_query = position.reshape(query_rows, per_query)
    owner = slot_ids == by_query[:, 0].reshape(1, -1)
    for g in range(1, per_query):
        owner = owner | (slot_ids == by_query[:, g].reshape(1, -1))
    owner = owner.astype(jnp.bfloat16)
    slot_block = (slot_ids % slots_each) // MOSTB

    send_queries = jnp.dot(owner, query, preferred_element_type=jnp.float32).astype(jnp.bfloat16)
    got_queries = lax.all_to_all(
        send_queries.reshape(n_corpus, slots_each, cols), "corpus", 0, 0, tiled=True
    ).reshape(slot_total, cols)
    wide = lax.dot_general(
        got_queries, passages, (((1,), (1,)), ((), ())), preferred_element_type=jnp.float32
    )
    scores = wide[:, :ROWS]
    for j in range(1, blocks_here):
        scores = jnp.where(slot_block == j, wide[:, j * ROWS : (j + 1) * ROWS], scores)
    returned = lax.all_to_all(
        scores.reshape(n_corpus, slots_each, ROWS), "corpus", 0, 0, tiled=True
    ).reshape(slot_total, ROWS)

    picked = returned[position]
    offsets = cand_offset.reshape(picks, offset_count)
    row_ids = lax.broadcasted_iota(jnp.int32, (1, 1, ROWS), 2)
    chosen = offsets[:, :, None] == row_ids
    partial = jnp.sum(jnp.where(chosen, picked[:, None, :], 0.0), axis=2)
    total = partial.reshape(query_rows, per_query * offset_count)
    total = total + lax.ppermute(total, "tensor", [(0, 1), (1, 0), (2, 3), (3, 2)])
    total = total + lax.ppermute(total, "tensor", [(0, 2), (2, 0), (1, 3), (3, 1)])
    student = 50.0 * total

    cached = teacher.reshape(query_rows, per_query * offset_count)
    log_student = student - jax.nn.logsumexp(student, axis=1, keepdims=True)
    log_teacher = cached - jax.nn.logsumexp(cached, axis=1, keepdims=True)
    prob_teacher = jnp.exp(log_teacher)
    kl_loss = jnp.sum(prob_teacher * (log_teacher - log_student), axis=1)
    dscore = (50.0 * (jnp.exp(log_student) - prob_teacher)).astype(jnp.bfloat16)

    spread = jnp.sum(
        jnp.where(chosen, dscore.reshape(picks, offset_count, 1).astype(jnp.float32), 0.0), axis=1
    ).astype(jnp.bfloat16)
    dense = jnp.dot(place, spread, preferred_element_type=jnp.float32).astype(jnp.bfloat16)
    got_dense = lax.all_to_all(
        dense.reshape(n_corpus, slots_each, ROWS), "corpus", 0, 0, tiled=True
    ).reshape(slot_total, ROWS)
    expanded = jnp.concatenate(
        [jnp.where(slot_block == j, got_dense, jnp.bfloat16(0)) for j in range(blocks_here)], axis=1
    )
    block_part = jnp.dot(expanded, passages, preferred_element_type=jnp.float32).astype(jnp.bfloat16)
    arrived = lax.all_to_all(
        block_part.reshape(n_corpus, slots_each, cols), "corpus", 0, 0, tiled=True
    ).reshape(slot_total, cols)
    query_grad = lax.dot_general(
        owner, arrived, (((0,), (0,)), ((), ())), preferred_element_type=jnp.float32
    ).astype(jnp.bfloat16)

    grad_mine = lax.all_gather(query_grad, "corpus", axis=0, tiled=True)
    grad_theirs = lax.ppermute(grad_mine, "fsdp", SWAP)
    across = (((0,), (0,)), ((), ()))
    head_grad = lax.dot_general(
        all_mine, grad_mine, across, preferred_element_type=jnp.float32
    ) + lax.dot_general(all_theirs, grad_theirs, across, preferred_element_type=jnp.float32)
    return (kl_loss, head_grad)


def solution(mesh):
    placed = (
        P(("corpus", "fsdp"), None),
        P("fsdp", "tensor"),
        P("corpus", "tensor"),
        P(("corpus", "fsdp"), None, None),
        P(("corpus", "fsdp"), None),
        P(("corpus", "fsdp"), None, None),
        P(),
    )
    return jax.shard_map(
        on_device,
        mesh=mesh,
        in_specs=placed,
        out_specs=(P(("corpus", "fsdp")), P("fsdp", "tensor")),
        check_vma=False,
    )
```

time: 657 us -> 354 us (0.54)
  local copies, waits for them, and re-layouts: 300 us -> 2.67 us
  waiting for transfers between devices: 269 us -> 230 us
  matrix products: 15.9 us -> 46.7 us
  blocking collectives: 37.5 us -> 22 us
  other arithmetic: 7.89 us -> 17.3 us
  starting transfers between devices: 11 us -> 20.2 us
    psum x2 -> x0, waiting for transfers between devices: 185 us -> none  [the longest x1 147 us: on_device(): head_grad = lax.psum(grad_share, 'corpus')]
    all_gather x1 -> x3, waiting for transfers between devices: 24.3 us -> 177 us  [the longest x1 72.7 us: on_device(): all_mine = lax.all_gather(mine, 'corpus', axis=0, tiled=True)]
    gather x7 -> x1, local copies, waits for them, and re-layouts: 153 us -> 1.03 us  [on_device(): picked = returned[position]]
    scatter x2 -> x0, local copies, waits for them, and re-layouts: 117 us -> none  [the longest x1 113 us: on_device(): jnp.zeros((slot_total * ROWS,), jnp.bfloat16).at[flat_index]]
    dot_general x4 -> x9, matrix products: 15.9 us -> 46.7 us  [the longest x1 16 us: on_device(): lax.dot_general(all_theirs, grad_theirs, across, preferred_element_type=j...]
    reduce_scatter x1 -> x0, waiting for transfers between devices: 24.9 us -> none  [on_device(): lax.psum_scatter(lax.dot_general(columns, query_grad, (((0,), (0,)), ((),...]
    reshape x10 -> x2, local copies, waits for them, and re-layouts: 15.7 us -> 0.2 us  [on_device(): total = partial.reshape(query_rows, per_query * offset_count)]
    all_to_all x2 -> x1, blocking collectives: 37.5 us -> 22 us  [on_device(): lax.all_to_all(block_part.reshape(n_corpus, slots_each, cols), 'corpus',...]
  transfers between devices with their start and end apart: 6 -> 11, of which waited for: 6 -> 10; matrix products, arithmetic and copies ran while one was open for 1% -> 5% of each run, Pallas kernels for 0% -> 0%
where the time goes in v1:
time: 354 us; the launch traced here: 353 us
  waiting for transfers between devices  230 us (65%)
  matrix products  46.7 us (13%)
  blocking collectives  22 us (6%)
  starting transfers between devices  20.2 us (6%)
  other arithmetic  17.3 us (5%)
  between operations  14 us (4%)
    all_gather x1, waiting for transfers between devices, on_device(): all_mine = lax.all_gather(mine, 'corpus', axis=0, tiled=True)  72.7 us
    all_gather x1, waiting for transfers between devices, on_device(): all_theirs = lax.all_gather(theirs, 'corpus', axis=0, tiled=True)  58.1 us
    all_gather x1, waiting for transfers between devices, on_device(): grad_mine = lax.all_gather(query_grad, 'corpus', axis=0, tiled=True)  46.6 us
    all_to_all x1, waiting for transfers between devices, on_device(): lax.all_to_all(send_queries.reshape(n_corpus, slots_each, cols), 'corpus'...  25.1 us
    all_to_all x1, blocking collectives, on_device(): lax.all_to_all(block_part.reshape(n_corpus, slots_each, cols), 'corpus',...  22 us
    dot_general x1, matrix products, on_device(): lax.dot_general(all_theirs, grad_theirs, across, preferred_element_type=j...  16 us
    dot_general x1, matrix products, on_device(): lax.dot_general(all_mine, grad_mine, across, preferred_element_type=jnp.f...  14.6 us
    all_to_all x1, waiting for transfers between devices, on_device(): lax.all_to_all(scores.reshape(n_corpus, slots_each, ROWS), 'corpus', 0, 0...  9.56 us
  transfers between devices with their start and end apart: 11, of which 10 were waited for; matrix products, arithmetic and copies ran while one was open for 5% of the time, Pallas kernels for 0%

profile of v1, /device:TPU:0, one launch (start us, length us, event | category | flops | bytes accessed | tf_op | source)
XLA Modules:
  0.0 353.1 jit_solution(15698942265412292982)
XLA Ops:
  7.2 2.2 broadcast_select_fusion
  9.6 1.9 collective-permute-done
  11.5 3.9 %fusion.26 = f32[128,1024]{1,0:T(8,128)} fusion(bf16[128,2048]{1,0:T(8,128)(2,1)S(1)} %collective-permute-done, bf16[2048,1024]{1,0:T(8,128)(2,1)} %param.8), kind=kOutput, calls=%fused_computation.91 | convolution fusion | flops 536870912 | bytes 5242880 | tf_op jit(solution)/shard_map/dot_general | solution.py:29
  16.5 1.2 collective-permute-done.1
  17.7 4.6 %convolution_convert_fusion = bf16[768,1024]{1,0:T(8,128)(2,1)} fusion(f32[128,1024]{1,0:T(8,128)} %collective-permute-done.1, s32[128]{0:T(128)S(1)} %get-tuple-element.3, s32[128]{0:T(128)S(1)} %get-tuple-element.4, s32[128]{0:T(128)S(1)} %get-tuple-element.5, s32[128]{0:T(128)S(1)} %get-tuple-element.2, bf16[128,2048]{1,0:T(8,128)(2,1)S(1)} %get-tuple-element.9, ...), kind=kOutput, calls=%fused_computation.5 | convolution fusion | flops 739934208 | bytes 6817792 | tf_op jit(solution)/shard_map/dot_general | solution.py:57
  22.3 8.2 %all-to-all-start = ((bf16[16,48,1024]{2,1,0:T(8,128)(2,1)}), bf16[16,48,1024]{2,1,0:T(8,128)(2,1)}, u32[]{:S(2)}, u32[]{:S(2)}) async-start(bf16[16,48,1024]{2,1,0:T(8,128)(2,1)} %bitcast.46), calls=%async_computation | async-start | bytes 3145728 | tf_op jit(solution)/shard_map/all_to_all | solution.py:58
  30.6 25.1 %all-to-all-done = bf16[16,48,1024]{2,1,0:T(8,128)(2,1)} async-done(((bf16[16,48,1024]{2,1,0:T(8,128)(2,1)}), bf16[16,48,1024]{2,1,0:T(8,128)(2,1)}, u32[]{:S(2)}, u32[]{:S(2)}) %all-to-all-start) | async-done | bytes 1572896 | tf_op jit(solution)/shard_map/all_to_all | solution.py:58
  55.7 3.2 fusion.27
  58.9 2.1 fusion.9
  61.1 3.6 %all-to-all-start.1 = ((f32[16,48,128]{2,1,0:T(8,128)}), f32[16,48,128]{2,1,0:T(8,128)S(1)}, u32[]{:S(2)}, u32[]{:S(2)}) async-start(f32[16,48,128]{2,1,0:T(8,128)} %bitcast.4), calls=%async_computation.1 | async-start | bytes 786432 | tf_op jit(solution)/shard_map/all_to_all | solution.py:67
  64.9 9.6 %all-to-all-done.1 = f32[16,48,128]{2,1,0:T(8,128)S(1)} async-done(((f32[16,48,128]{2,1,0:T(8,128)}), f32[16,48,128]{2,1,0:T(8,128)S(1)}, u32[]{:S(2)}, u32[]{:S(2)}) %all-to-all-start.1) | async-done | bytes 393248 | tf_op jit(solution)/shard_map/all_to_all | solution.py:67
  74.4 1.0 gather_fusion
  75.5 5.1 %select_reduce_fusion.1 = f32[512,32]{1,0:T(8,128)S(1)} fusion(f32[512,128]{1,0:T(8,128)S(1)} %gather_fusion, s32[512,32]{1,0:T(8,128)S(1)} %bitcast.47), kind=kLoop, calls=%fused_computation.2 | loop fusion | flops 6275072 | bytes 393216 | tf_op jit(solution)/shard_map/reduce_sum | solution.py:75
  80.8 1.6 collective-permute-start.2
  82.4 2.7 collective-permute-done.2
  85.2 3.1 collective-permute-start.3
  88.3 2.7 collective-permute-done.3
  91.9 5.6 %select_reduce_fusion = bf16[512,128]{1,0:T(8,128)(2,1)S(1)} fusion(f32[512,32]{1,0:T(8,128)S(1)} %reshape.201, s32[512,32]{1,0:T(8,128)S(1)} %bitcast.48), kind=kLoop, calls=%fused_computation.1 | loop fusion | flops 6225920 | bytes 262144 | tf_op jit(solution)/shard_map/reduce_sum | solution.py:88
  97.5 1.1 fusion.1
  98.6 3.5 all-to-all-start.2
  102.2 8.2 %all-to-all-done.2 = bf16[16,48,128]{2,1,0:T(8,128)(2,1)S(1)} async-done(((bf16[16,48,128]{2,1,0:T(8,128)(2,1)}), bf16[16,48,128]{2,1,0:T(8,128)(2,1)S(1)}, u32[]{:S(2)}, u32[]{:S(2)}) %all-to-all-start.2) | async-done | bytes 196640 | tf_op jit(solution)/shard_map/all_to_all | solution.py:92
  110.4 1.2 bitcast_select_fusion
  112.1 1.8 convolution_convert_fusion.1
  114.0 22.0 %all_to_all.20 = bf16[16,48,1024]{2,1,0:T(8,128)(2,1)S(1)} all-to-all(bf16[16,48,1024]{2,1,0:T(8,128)(2,1)S(1)} %bitcast.50), channel_id=1, replica_groups=mesh['corpus'=16,'fsdp'=2,'tensor'=4] {'corpus'}, dimensions={0} | all-to-all | bytes 3145728 | tf_op jit(solution)/shard_map/all_to_all | solution.py:99
  136.0 1.2 convolution_convert_fusion.2
  137.2 0.7 all-gather.4.cloned.1.call-update
  138.0 0.7 all-gather.8.cloned.1.call-update
  138.7 46.6 %all-gather.6.cloned.1.call-done = bf16[2048,1024]{1,0:T(8,128)(2,1)} async-done(((bf16[128,1024]{1,0:T(8,128)(2,1)}), bf16[2048,1024]{1,0:T(8,128)(2,1)}) %all-gather.6.cloned.1.call-update) | async-done | bytes 4194320 | tf_op jit(solution)/shard_map/all_gather | solution.py:106
  185.2 72.7 %all-gather.4.cloned.1.call-done = bf16[2048,2048]{1,0:T(8,128)(2,1)} async-done(((bf16[128,2048]{1,0:T(8,128)(2,1)}), bf16[2048,2048]{1,0:T(8,128)(2,1)}) %all-gather.4.cloned.1.call-update) | async-done | bytes 8388624 | tf_op jit(solution)/shard_map/all_gather | solution.py:33
  257.9 14.6 %fusion.28 = f32[2048,1024]{1,0:T(8,128)} fusion(bf16[2048,2048]{1,0:T(8,128)(2,1)} %all-gather.4.cloned.1.call-done, bf16[2048,1024]{1,0:T(8,128)(2,1)} %all-gather.6.cloned.1.call-done), kind=kOutput, calls=%fused_computation.93 | convolution fusion | flops 8589934592 | bytes 20971520 | tf_op jit(solution)/shard_map/dot_general | solution.py:109
  272.6 58.1 %all-gather.8.cloned.1.call-done = bf16[2048,2048]{1,0:T(8,128)(2,1)} async-done(((bf16[128,2048]{1,0:T(8,128)(2,1)}), bf16[2048,2048]{1,0:T(8,128)(2,1)}) %all-gather.8.cloned.1.call-update) | async-done | bytes 8388624 | tf_op jit(solution)/shard_map/all_gather | solution.py:34
  330.6 16.0 %convolution_add_fusion = f32[2048,1024]{1,0:T(8,128)} fusion(f32[2048,1024]{1,0:T(8,128)} %fusion.28, bf16[2048,2048]{1,0:T(8,128)(2,1)} %all-gather.8.cloned.1.call-done, bf16[2048,1024]{1,0:T(8,128)(2,1)} %collective-permute-done.4), kind=kOutput, calls=%fused_computation.4 | convolution fusion | flops 8592031744 | bytes 29360128 | tf_op jit(solution)/shard_map/dot_general | solution.py:111
  (61 shorter events, 3.4 us)
Async XLA Ops:
  7.2 48.5 %copy-start = (bf16[1024,1024]{1,0:T(8,128)(2,1)S(1)}, bf16[1024,1024]{1,0:T(8,128)(2,1)}, u32[]{:S(2)}) copy-start(bf16[1024,1024]{1,0:T(8,128)(2,1)} %param.9) | copy-start | bytes 6291460
  7.2 2.2 copy-start.6
  9.4 8.3 %copy-start.2 = (bf16[128,2048]{1,0:T(8,128)(2,1)}, bf16[128,2048]{1,0:T(8,128)(2,1)S(1)}, u32[]{:S(2)}) copy-start(bf16[128,2048]{1,0:T(8,128)(2,1)S(1)} %get-tuple-element.9) | copy-start | bytes 1572868
  9.4 2.1 collective-permute-start
  11.5 3.9 %copy-start.3 = (bf16[128,2048]{1,0:T(8,128)(2,1)}, bf16[128,2048]{1,0:T(8,128)(2,1)S(1)}, u32[]{:S(2)}) copy-start(bf16[128,2048]{1,0:T(8,128)(2,1)S(1)} %collective-permute-done) | copy-start | bytes 1572868
  11.5 4.1 %copy-start.7 = (s32[128]{0:T(128)S(1)}, s32[128]{0:T(128)}, u32[]{:S(2)}) copy-start(s32[128]{0:T(128)} %param.13) | copy-start | bytes 1540
  15.5 2.3 collective-permute-start.1
  22.3 33.4 %all-to-all-start = ((bf16[16,48,1024]{2,1,0:T(8,128)(2,1)}), bf16[16,48,1024]{2,1,0:T(8,128)(2,1)}, u32[]{:S(2)}, u32[]{:S(2)}) async-start(bf16[16,48,1024]{2,1,0:T(8,128)(2,1)} %bitcast.46), calls=%async_computation | async-start | bytes 3145728 | tf_op jit(solution)/shard_map/all_to_all | solution.py:58
  58.9 5.7 %copy-start.5 = (s32[128,4,32]{0,2,1:T(8,128)S(1)}, s32[128,4,32]{0,2,1:T(8,128)}, u32[]{:S(2)}) copy-start(s32[128,4,32]{0,2,1:T(8,128)} %param.12) | copy-start | bytes 196612
  58.9 5.9 %copy-start.4 = (f32[128,4,32]{0,2,1:T(8,128)S(1)}, f32[128,4,32]{0,2,1:T(8,128)}, u32[]{:S(2)}) copy-start(f32[128,4,32]{0,2,1:T(8,128)} %param.10) | copy-start | bytes 196612
  61.1 13.4 %all-to-all-start.1 = ((f32[16,48,128]{2,1,0:T(8,128)}), f32[16,48,128]{2,1,0:T(8,128)S(1)}, u32[]{:S(2)}, u32[]{:S(2)}) async-start(f32[16,48,128]{2,1,0:T(8,128)} %bitcast.4), calls=%async_computation.1 | async-start | bytes 786432 | tf_op jit(solution)/shard_map/all_to_all | solution.py:67
  80.8 4.3 %collective-permute-start.2 = (f32[128,128]{0,1:T(8,128)S(1)}, f32[128,128]{0,1:T(8,128)S(1)}, u32[]{:S(2)}, u32[]{:S(2)}) collective-permute-start(f32[128,128]{0,1:T(8,128)S(1)} %copy.20), channel_id=1, source_target_pairs={{0,1},{1,0},{2,3},{3,2},{4,5},{5,4},{6,7},{7,6},{8,9},{9,8},{10,11... | collective-permute-start | bytes 196616 | tf_op jit(solution)/shard_map/ppermute | solution.py:77
  85.2 5.8 %collective-permute-start.3 = (f32[128,128]{0,1:T(8,128)S(1)}, f32[128,128]{0,1:T(8,128)S(1)}, u32[]{:S(2)}, u32[]{:S(2)}) collective-permute-start(f32[128,128]{0,1:T(8,128)S(1)} %add.157), channel_id=1, source_target_pairs={{0,2},{2,0},{1,3},{3,1},{4,6},{6,4},{5,7},{7,5},{8,10},{10,8},{9,1... | collective-permute-start | bytes 196616 | tf_op jit(solution)/shard_map/ppermute | solution.py:78
  98.6 11.8 %all-to-all-start.2 = ((bf16[16,48,128]{2,1,0:T(8,128)(2,1)}), bf16[16,48,128]{2,1,0:T(8,128)(2,1)S(1)}, u32[]{:S(2)}, u32[]{:S(2)}) async-start(bf16[16,48,128]{2,1,0:T(8,128)(2,1)} %bitcast.8), calls=%async_computation.2 | async-start | bytes 393216 | tf_op jit(solution)/shard_map/all_to_all | solution.py:92
  102.1 83.1 %all-gather.6.cloned.1.call-start = ((), (), s32[]{:S(2)}) async-start(), calls=%async_computation.5 | async-start | bytes 4456448 | tf_op jit(solution)/shard_map/all_gather | solution.py:106
  137.2 120.7 %all-gather.4.cloned.1.call-start = ((), (), s32[]{:S(2)}) async-start(), calls=%async_computation.4 | async-start | bytes 8912896 | tf_op jit(solution)/shard_map/all_gather | solution.py:33
  137.9 192.7 %all-gather.8.cloned.1.call-start = ((), (), s32[]{:S(2)}) async-start(), calls=%async_computation.6 | async-start | bytes 8912896 | tf_op jit(solution)/shard_map/all_gather | solution.py:34
  185.2 145.4 %collective-permute-start.4 = (bf16[2048,1024]{1,0:T(8,128)(2,1)}, bf16[2048,1024]{1,0:T(8,128)(2,1)}, u32[]{:S(2)}, u32[]{:S(2)}) collective-permute-start(bf16[2048,1024]{1,0:T(8,128)(2,1)} %all-gather.6.cloned.1.call-done), channel_id=1, source_target_pairs={{0,4},{4,0},{1,5},{5,1},{2,6},{6,2},{3,7},{7,3},{8,12},{12,8},{9,1... | collective-permute-start | bytes 12582920 | tf_op jit(solution)/shard_map/ppermute | solution.py:107
  330.6 16.0 %copy-start.1 = (bf16[1024,1024]{1,0:T(8,128)(2,1)S(1)}, bf16[1024,1024]{1,0:T(8,128)(2,1)}, u32[]{:S(2)}) copy-start(bf16[1024,1024]{1,0:T(8,128)(2,1)} %param.9) | copy-start | bytes 6291460
Sparse Core Ops, SparseCore 0:
  137.3 47.8 all-gather.5
  187.4 70.5 all-gather.3
  260.1 70.5 all-gather.7
